TPU v7x, 32 devices: a whole 2x2x4 slice. The times are simulated.
32 devices in a mesh: aa: 4 (over z), ba: 8 (over y, x, core).
Axes of the slice: x: 2, y: 2, z: 4, core: 2. Of those that a mesh axis runs over, the one named last changes fastest.
Arguments:
- atom_cond: float32 [12288, 128], P(('aa', 'ba')), may hold values from -6 to 6
- noisy_pos: float32 [3, 12288], P(None, ('aa', 'ba')), may hold values from -8 to 8
- noise_level: float32 [1], replicated, may hold values from 0.1 to 4
- atom_token: int32 [12288], P(('aa', 'ba')), may hold values from -1 to 1023, as said below
- token_cond: float32 [1024, 768], P('aa'), may hold values from -6 to 6
- pair: bfloat16 [1024, 1024, 128], P('aa', 'ba'), may hold values from -64 to 64
- pair_bias_weight: bfloat16 [16, 128], replicated, may hold values from -0.375 to 0.375
- gains: float32 [3, 768], replicated, may hold values from 0.25 to 1.75
- w_pos: float32 [3, 128], replicated, may hold values from -3.5 to 3.5
- w_atom_token: bfloat16 [128, 768], replicated, may hold values from -0.5 to 0.5
- w_query_gate: bfloat16 [768, 1536], replicated, may hold values from -0.21875 to 0.21875
- w_key_value: bfloat16 [768, 1536], replicated, may hold values from -0.21875 to 0.21875
- w_attn_out: bfloat16 [768, 768], replicated, may hold values from -0.21875 to 0.21875
- w_up: bfloat16 [768, 3072], replicated, may hold values from -0.21875 to 0.21875
- w_down: bfloat16 [1536, 768], replicated, may hold values from -0.15625 to 0.15625
- w_token_atom: bfloat16 [768, 128], replicated, may hold values from -0.21875 to 0.21875
- w_pos_out: bfloat16 [3, 128], replicated, may hold values from -0.5 to 0.5
Outputs:
- denoised: float32 [3, 12288], P(None, ('aa', 'ba'))
- token_out: float32 [1024, 768], P('aa')
Inputs may be any that keep to these rules, and one draw needn't show every extreme that they name: `atom_token`: atom slots come in 4 groups of 3072 consecutive slots; group r holds only atoms of tokens r * 256 to (r + 1) * 256 - 1, in nondecreasing token order, live slots first and -1 after them. Every token has 1 to 12 atoms, and some token of every group has exactly 12.
All inputs are finite; a program needn't handle non-finite values.
Results may differ from a plain program's by a relative error of at most 0.01.
Values may be sent and summed in bfloat16 or wider, within the bound.
A program may use at most 128 MiB of HBM per device.

v0:
```python
import jax
import jax.numpy as jnp
from jax import lax
from jax.sharding import PartitionSpec as P

D = 768
HEADS = 16


def broadcast(value, axis, source):
    kept = jnp.where(lax.axis_index(axis) == source, value, 0).astype(value.dtype)
    return lax.psum(kept, axis)


def layer_norm(values, gain_row):
    mean_value = jnp.mean(values, axis=-1, keepdims=True)
    centered = values - mean_value
    variance = jnp.mean(centered * centered, axis=-1, keepdims=True)
    return centered * lax.rsqrt(variance + 1e-05) * gain_row


def widen(factor, head_dim):
    return jnp.repeat(factor.T, head_dim, axis=1)


def token_sums(local_ids, rounded_state, w_atom_token, tok_rows):
    selector = (local_ids[:, None] == jnp.arange(tok_rows, dtype=jnp.int32)[None, :]).astype(
        jnp.bfloat16
    )
    hidden_atom = jax.nn.relu(
        jnp.dot(rounded_state, w_atom_token, preferred_element_type=jnp.float32)
    ).astype(jnp.bfloat16)
    sums = lax.dot_general(
        selector, hidden_atom, (((0,), (0,)), ((), ())), preferred_element_type=jnp.float32
    )
    return (sums, jnp.sum(selector.astype(jnp.float32), axis=0))


def project_start(tokens_start, gains, w_query_gate):
    normed = layer_norm(tokens_start, gains[0]).astype(jnp.bfloat16)
    query_gate = jnp.dot(normed, w_query_gate, preferred_element_type=jnp.float32)
    width = query_gate.shape[1] // 2
    query_rows = query_gate[:, :width].astype(jnp.bfloat16)
    gate_value = jax.nn.sigmoid(query_gate[:, width:]).astype(jnp.bfloat16)
    return (normed, query_rows, gate_value)


def on_device(
    atom_cond,
    noisy_pos,
    noise_level,
    atom_token,
    token_cond,
    pair,
    pair_bias_weight,
    gains,
    w_pos,
    w_atom_token,
    w_query_gate,
    w_key_value,
    w_attn_out,
    w_up,
    w_down,
    w_token_atom,
    w_pos_out,
):
    tok_rows = token_cond.shape[0]
    block_cols = pair.shape[1]
    head_dim = D // HEADS
    row_index = lax.axis_index("aa")
    col_index = lax.axis_index("ba")
    noise_sigma = noise_level[0]
    inv_scale = 1.0 / jnp.sqrt(noise_sigma * noise_sigma + 1.0)
    scaled_pos = noisy_pos * inv_scale
    atom_state = atom_cond + scaled_pos[0][:, None] * w_pos[0]
    atom_state = atom_state + scaled_pos[1][:, None] * w_pos[1]
    atom_state = atom_state + scaled_pos[2][:, None] * w_pos[2]
    rounded_state = atom_state.astype(jnp.bfloat16)
    local_token = atom_token - row_index * tok_rows
    one_hot = (local_token[:, None] == jnp.arange(tok_rows, dtype=jnp.int32)[None, :]).astype(
        jnp.bfloat16
    )
    group_state, group_ids = (
        lax.all_gather(rounded_state, "ba", axis=0, tiled=True),
        lax.all_gather(atom_token, "ba", axis=0, tiled=True),
    )
    summed, counts = token_sums(
        group_ids - row_index * tok_rows, group_state, w_atom_token, tok_rows
    )
    tokens_start = token_cond + summed / counts[:, None]
    normed, query_rows, gate_value = project_start(tokens_start, gains, w_query_gate)
    offset_row = col_index * block_cols % tok_rows
    owner_row = col_index * block_cols // tok_rows
    slice_rows = lax.dynamic_slice_in_dim(normed, offset_row, block_cols, 0)
    kv_local = jnp.dot(slice_rows, w_key_value, preferred_element_type=jnp.float32).astype(
        jnp.bfloat16
    )
    key_value = broadcast(kv_local, "aa", owner_row)
    key_heads = key_value[:, :D].reshape(block_cols, HEADS, head_dim)
    value_heads = key_value[:, D:].reshape(block_cols, HEADS, head_dim)
    query_heads = query_rows.reshape(tok_rows, HEADS, head_dim)
    scores = jnp.einsum(
        "ihd,jhd->hij", query_heads, key_heads, preferred_element_type=jnp.float32
    ) * head_dim ** (-0.5) + jnp.einsum(
        "hc,ijc->hij", pair_bias_weight, pair, preferred_element_type=jnp.float32
    )
    block_max = jnp.max(scores, axis=2)
    weights = jnp.exp(scores - block_max[:, :, None])
    block_total = jnp.sum(weights, axis=2)
    partial_out = jnp.einsum(
        "hij,jhd->ihd",
        weights.astype(jnp.bfloat16),
        value_heads,
        preferred_element_type=jnp.float32,
    ).reshape(tok_rows, D)
    overall = lax.pmax(block_max, "ba")
    factor = jnp.exp(block_max - overall)
    out_all, total_all = (
        lax.psum((partial_out * widen(factor, head_dim)).astype(jnp.bfloat16), "ba").astype(
            jnp.float32
        ),
        lax.psum((block_total * factor).astype(jnp.bfloat16), "ba").astype(jnp.float32),
    )
    attended = out_all / widen(total_all, head_dim)
    mixed_heads = (attended * gate_value.astype(jnp.float32)).astype(jnp.bfloat16)
    tokens_mid = tokens_start + jnp.dot(mixed_heads, w_attn_out, preferred_element_type=jnp.float32)
    normed_mid = layer_norm(tokens_mid, gains[1]).astype(jnp.bfloat16)
    gate_up = jnp.dot(normed_mid, w_up, preferred_element_type=jnp.float32)
    hidden_units = w_down.shape[0]
    inner_units = (jax.nn.silu(gate_up[:, :hidden_units]) * gate_up[:, hidden_units:]).astype(
        jnp.bfloat16
    )
    token_out = tokens_mid + jnp.dot(inner_units, w_down, preferred_element_type=jnp.float32)
    normed_out = layer_norm(token_out, gains[2]).astype(jnp.bfloat16)
    token_atom = jnp.dot(normed_out, w_token_atom, preferred_element_type=jnp.float32).astype(
        jnp.bfloat16
    )
    picked = jnp.dot(one_hot, token_atom, preferred_element_type=jnp.float32)
    atom_final = atom_state + picked
    atom_normed = layer_norm(atom_final, 1.0).astype(jnp.bfloat16)
    update = lax.dot_general(
        w_pos_out, atom_normed, (((1,), (1,)), ((), ())), preferred_element_type=jnp.float32
    )
    denoised = noisy_pos * (inv_scale * inv_scale) + update * (noise_sigma * inv_scale)
    return (denoised, token_out)


def solution(mesh):
    in_specs = (
        P(("aa", "ba"), None),
        P(None, ("aa", "ba")),
        P(),
        P(("aa", "ba")),
        P("aa", None),
        P("aa", "ba", None),
        P(),
        P(),
        P(),
        P(),
        P(),
        P(),
        P(),
        P(),
        P(),
        P(),
        P(),
    )
    out_specs = (P(None, ("aa", "ba")), P("aa", None))
    return jax.shard_map(
        on_device, mesh=mesh, in_specs=in_specs, out_specs=out_specs, check_vma=False
    )
```

profile of v0, /device:TPU:0, one launch (start us, length us, event | category | flops | bytes accessed | tf_op | source)
XLA Modules:
  0.0 193.1 jit_solution(8978866109593761856)
XLA Ops:
  8.1 10.4 %all-gather = s32[8,1,384]{2,1,0:T(1,128)S(1)} all-gather(s32[1,1,384]{2,1,0:T(1,128)S(1)} %reshape.81), channel_id=1, replica_groups=mesh['aa'=4,'ba'=8] {'ba'}, dimensions={0}, use_global_device_ids=true | all-gather | bytes 13824 | tf_op jit(solution)/shard_map/all_gather | solution.py:85
  18.5 1.4 convert_reduce_fusion
  23.3 12.2 %all_gather.7 = bf16[3072,128]{0,1:T(8,128)(2,1)} all-gather(bf16[384,128]{0,1:T(8,128)(2,1)S(1)} %fusion.33), channel_id=1, replica_groups=mesh['aa'=4,'ba'=8] {'ba'}, dimensions={0}, use_global_device_ids=true | all-gather | bytes 884736 | tf_op jit(solution)/shard_map/all_gather | solution.py:84
  35.5 1.4 slice_reduce_fusion
  37.0 5.9 %fusion.45 = (f32[256]{0:T(256)S(1)}, f32[256,768]{1,0:T(8,128)S(1)}) fusion(f32[256,768]{1,0:T(8,128)} %param.21, f32[256]{0:T(256)S(1)} %convert_reduce_fusion, bf16[3072,128]{0,1:T(8,128)(2,1)} %all_gather.7, bf16[128,768]{1,0:T(8,128)(2,1)} %param.26, s32[3072]{0:T(1024)S(1)} %bitcast.55), kind=kOutput, calls=%fused_computation.88 | convolution fusion | flops 1818033920 | bytes 2570240 | tf_op jit(solution)/shard_map/dot_general | solution.py:33
  43.3 2.9 %fusion.2 = bf16[128,1536]{1,0:T(8,128)(2,1)} fusion(bf16[768,1536]{1,0:T(8,128)(2,1)} %param.28, pred[]{:T(512)S(6)} %eq.37, bf16[256,768]{1,0:T(8,128)(2,1)S(1)} %multiply_convert_fusion.3, s32[]{:T(128)S(6)} %select_n.25), kind=kOutput, calls=%fused_computation.6 | convolution fusion | flops 302383104 | bytes 2949125 | tf_op jit(solution)/shard_map/dot_general | solution.py:95
  46.3 7.0 %fusion.38 = f32[16,256,128]{2,0,1:T(8,128)} fusion(bf16[256,128,128]{2,1,0:T(8,128)(2,1)} %param.22, bf16[16,128]{1,0:T(8,128)(2,1)S(1)} %copy-done.12), kind=kOutput, calls=%fused_computation.62 | convolution fusion | flops 134217728 | bytes 10489856 | tf_op jit(solution)/shard_map/hc,ijc->hij/dot_general | solution.py:104
  53.3 2.9 %copy.47 = f32[16,256,128]{1,2,0:T(8,128)} copy(f32[16,256,128]{2,0,1:T(8,128)} %fusion.38) | data formatting | bytes 4194304 | tf_op jit(solution)/shard_map/hc,ijc->hij/dot_general | solution.py:104
  58.9 1.2 copy.45
  60.1 23.5 %all-reduce.3.cloned.1.call-done = bf16[128,1536]{1,0:T(8,128)(2,1)} async-done(((bf16[128,1536]{1,0:T(8,128)(2,1)}), bf16[128,1536]{1,0:T(8,128)(2,1)}) %all-reduce.3.cloned.1.call-update) | async-done | bytes 393232 | tf_op jit(solution)/shard_map/psum | solution.py:12
  83.6 1.8 fusion.44
  85.4 1.8 copy.46
  87.2 3.6 %fusion.46 = (f32[16,256]{1,0:T(8,128)S(1)}, f32[16,256,128]{1,2,0:T(8,128)}) fusion(f32[16,256,128]{1,2,0:T(8,128)} %copy.47, bf16[256,16,48]{0,2,1:T(8,128)(2,1)S(1)} %bitcast.50, bf16[128,16,48]{0,2,1:T(8,128)(2,1)} %bitcast.52), kind=kOutput, calls=%fused_computation.89 | convolution fusion | flops 51900416 | bytes 4800512 | tf_op jit(solution)/shard_map/ihd,jhd->hij/dot_general | solution.py:102
  90.7 22.6 %pmax.7 = f32[16,256]{1,0:T(8,128)S(1)} all-reduce(f32[16,256]{1,0:T(8,128)S(1)} %get-tuple-element.17), channel_id=1, replica_groups=mesh['aa'=4,'ba'=8] {'ba'}, use_global_device_ids=true, to_apply=%region_5.6 | all-reduce | flops 4096 | bytes 32768 | tf_op jit(solution)/shard_map/pmax | solution.py:116
  113.3 1.9 fusion.3
  116.6 2.2 %fusion.8 = bf16[256,16,48]{0,2,1:T(8,128)(2,1)S(1)} fusion(bf16[128,16,48]{0,2,1:T(8,128)(2,1)} %bitcast.53, f32[16,256,128]{1,2,0:T(8,128)} %get-tuple-element.18, f32[16,256]{1,0:T(8,128)S(1)} %get-tuple-element.17, f32[256,16]{0,1:T(8,128)S(1)} %get-tuple-element.10), kind=kOutput, calls=%fused_computation.18 | convolution fusion | flops 51773440 | bytes 2719744 | tf_op jit(solution)/shard_map/hij,jhd->ihd/dot_general | solution.py:110
  119.8 1.3 broadcast_subtract_fusion.1
  121.1 12.5 %psum.23 = bf16[256,16]{0,1:T(8,128)(2,1)S(1)} all-reduce(bf16[256,16]{0,1:T(8,128)(2,1)} %get-tuple-element.11), channel_id=1, replica_groups=mesh['aa'=4,'ba'=8] {'ba'}, use_global_device_ids=true, to_apply=%region_8.9 | all-reduce | flops 4096 | bytes 16384 | tf_op jit(solution)/shard_map/psum | solution.py:122
  134.5 2.3 %copy.50 = f32[256,768]{1,0:T(8,128)} copy(f32[256,768]{0,1:T(8,128)} %bitcast.49) | data formatting | bytes 1572864 | tf_op jit(solution)/shard_map/reshape | solution.py:23
  136.8 36.3 %all-reduce.5.cloned.1.call-done = bf16[256,768]{1,0:T(8,128)(2,1)} async-done(((bf16[256,768]{1,0:T(8,128)(2,1)}), bf16[256,768]{1,0:T(8,128)(2,1)}) %all-reduce.5.cloned.1.call-update) | async-done | bytes 393232 | tf_op jit(solution)/shard_map/psum | solution.py:119
  173.1 2.6 %fusion.47 = (f32[256]{0:T(256)S(1)}, f32[256,768]{1,0:T(8,128)S(1)}) fusion(f32[256,768]{1,0:T(8,128)S(1)} %get-tuple-element.16, bf16[768,768]{1,0:T(8,128)(2,1)} %param.29, f32[256,768]{1,0:T(8,128)} %copy.50, bf16[256,768]{1,0:T(8,128)(2,1)} %all-reduce.5.cloned.1.call-done, f32[256,1536]{1,0:T(8,128)} %copy-done.1), kind=kOutput, calls=%fused_computation.90 | convolution fusion | flops 304152320 | bytes 4719616 | tf_op jit(solution)/shard_map/dot_general | solution.py:126
  176.0 4.0 %fusion.20 = f32[256,3072]{1,0:T(8,128)S(1)} fusion(bf16[768,3072]{1,0:T(8,128)(2,1)} %param.30, f32[256,768]{1,0:T(8,128)S(1)} %get-tuple-element.20, f32[768]{0:T(1024)S(1)} %copy-done.14, f32[256]{0:T(256)S(1)} %add_rsqrt_fusion.2, f32[256]{0:T(256)S(1)} %broadcast_multiply_fusion.3), kind=kOutput, calls=%fused_computation.40 | convolution fusion | flops 1208745984 | bytes 8655872 | tf_op jit(solution)/shard_map/dot_general | solution.py:128
  181.9 2.1 %fusion.49 = (f32[384]{0:T(512)}, f32[384,128]{0,1:T(8,128)S(1)}) fusion(bf16[768,128]{1,0:T(8,128)(2,1)} %param.32, f32[256,768]{1,0:T(8,128)S(1)} %get-tuple-element.22, f32[768]{0:T(1024)} %get-tuple-element.2, f32[256]{0:T(256)} %add_rsqrt_fusion.1, f32[256]{0:T(256)} %copy-done.13, s32[384]{0:T(512)} %broadcast_subtract_fusion.1, f32[128]{0:T(128)} %copy-done.16, ...), kind=kOutput, calls=%fused_computation.92 | convolution fusion | flops 76807808 | bytes 1390592 | tf_op jit(solution)/shard_map/dot_general | solution.py:138
  184.8 1.4 fusion.12
  (69 shorter events, 13.0 us)
Async XLA Ops:
  7.2 49.0 %copy-start = (bf16[768,1536]{1,0:T(8,128)(2,1)S(1)}, bf16[768,1536]{1,0:T(8,128)(2,1)}, u32[]{:S(2)}) copy-start(bf16[768,1536]{1,0:T(8,128)(2,1)} %param.27) | copy-start | bytes 7077892
  7.2 76.4 %all-reduce.3.cloned.1.call-start = ((), (), s32[]{:S(2)}) async-start(), calls=%async_computation | async-start | bytes 786432 | tf_op jit(solution)/shard_map/psum | solution.py:12
  20.9 14.6 %copy-start.3 = (f32[384,128]{0,1:T(8,128)}, f32[384,128]{0,1:T(8,128)S(1)}, u32[]{:S(2)}) copy-start(f32[384,128]{0,1:T(8,128)S(1)} %copy.43) | copy-start | bytes 589828
  21.7 13.8 %copy-start.15 = (f32[128]{0:T(128)}, f32[128]{0:T(128)S(1)}, u32[]{:S(2)}) copy-start(f32[128]{0:T(128)S(1)} %get-tuple-element.12) | copy-start | bytes 1540
  21.7 13.8 %copy-start.16 = (f32[128]{0:T(128)}, f32[128]{0:T(128)S(1)}, u32[]{:S(2)}) copy-start(f32[128]{0:T(128)S(1)} %get-tuple-element.13) | copy-start | bytes 1540
  21.7 13.8 %copy-start.17 = (f32[128]{0:T(128)}, f32[128]{0:T(128)S(1)}, u32[]{:S(2)}) copy-start(f32[128]{0:T(128)S(1)} %get-tuple-element.14) | copy-start | bytes 1540
  23.1 12.4 %copy-start.7 = (f32[384]{0:T(512)}, f32[384]{0:T(512)S(1)}, u32[]{:S(2)}) copy-start(f32[384]{0:T(512)S(1)} %get-tuple-element.5) | copy-start | bytes 4612
  23.1 12.4 %copy-start.9 = (f32[384]{0:T(512)}, f32[384]{0:T(512)S(1)}, u32[]{:S(2)}) copy-start(f32[384]{0:T(512)S(1)} %get-tuple-element.6) | copy-start | bytes 4612
  23.2 12.4 %copy-start.11 = (f32[384]{0:T(512)}, f32[384]{0:T(512)S(1)}, u32[]{:S(2)}) copy-start(f32[384]{0:T(512)S(1)} %get-tuple-element.7) | copy-start | bytes 4612
  43.1 3.2 %copy-start.12 = (bf16[16,128]{1,0:T(8,128)(2,1)S(1)}, bf16[16,128]{1,0:T(8,128)(2,1)}, u32[]{:S(2)}) copy-start(bf16[16,128]{1,0:T(8,128)(2,1)} %param.23) | copy-start | bytes 12292
  46.2 126.9 %all-reduce.5.cloned.1.call-start = ((), (), s32[]{:S(2)}) async-start(), calls=%async_computation.1 | async-start | bytes 786432 | tf_op jit(solution)/shard_map/psum | solution.py:119
  57.0 1.2 copy-start.1
  90.7 24.5 %copy-start.5 = (bf16[128,768]{1,0:T(8,128)(2,1)S(1)}, bf16[128,768]{1,0:T(8,128)(2,1)}, u32[]{:S(2)}) copy-start(bf16[128,768]{1,0:T(8,128)(2,1)} %get-tuple-element.8) | copy-start | bytes 589828
  136.8 39.2 %copy-start.14 = (f32[768]{0:T(1024)S(1)}, f32[768]{0:T(1024)}, u32[]{:S(2)}) copy-start(f32[768]{0:T(1024)} %get-tuple-element.4) | copy-start | bytes 9220
  176.0 4.0 %copy-start.18 = (bf16[1536,768]{1,0:T(8,128)(2,1)S(1)}, bf16[1536,768]{1,0:T(8,128)(2,1)}, u32[]{:S(2)}) copy-start(bf16[1536,768]{1,0:T(8,128)(2,1)} %param.31) | copy-start | bytes 7077892
  180.0 1.9 copy-start.4
  180.0 1.9 copy-start.8
  180.0 1.9 copy-start.10
  181.1 5.1 %copy-start.2 = (f32[256,768]{1,0:T(8,128)}, f32[256,768]{1,0:T(8,128)S(1)}, u32[]{:S(2)}) copy-start(f32[256,768]{1,0:T(8,128)S(1)} %get-tuple-element.22) | copy-start | bytes 2359300
  181.1 3.7 %copy-start.6 = (f32[3,384]{1,0:T(4,128)S(1)}, f32[3,384]{1,0:T(4,128)}, u32[]{:S(2)}) copy-start(f32[3,384]{1,0:T(4,128)} %param.18) | copy-start | bytes 13828
  181.1 0.8 copy-start.13
Sparse Core Ops, SparseCore 0:
  46.3 37.2 all-reduce.2
  119.9 53.1 all-reduce.4
where the time goes:
time: 194 us; the launch traced here: 193 us
  waiting for transfers between devices  59.9 us (31%)
  blocking collectives  57.7 us (30%)
  matrix products  33.5 us (17%)
  local copies, waits for them, and re-layouts  18.8 us (10%)
  between operations  15.1 us (8%)
  other arithmetic  8.12 us (4%)
    psum x1, waiting for transfers between devices, on_device(): lax.psum((partial_out * widen(factor, head_dim)).astype(jnp.bfloat16), 'ba')  36.3 us
    psum x1, waiting for transfers between devices, broadcast(): return lax.psum(kept, axis)  23.5 us
    pmax x1, blocking collectives, on_device(): overall = lax.pmax(block_max, 'ba')  22.6 us
    psum x1, blocking collectives, on_device(): lax.psum((block_total * factor).astype(jnp.bfloat16), 'ba')  12.5 us
    all_gather x1, blocking collectives, on_device(): lax.all_gather(rounded_state, 'ba', axis=0, tiled=True)  12.2 us
    all_gather x1, blocking collectives, on_device(): lax.all_gather(atom_token, 'ba', axis=0, tiled=True)  10.4 us
    dot_general x1, matrix products, on_device(): jnp.einsum('hc,ijc->hij', pair_bias_weight, pair, preferred_element_type=...  6.97 us
    dot_general x1, matrix products, token_sums(): lax.dot_general(selector, hidden_atom, (((0,), (0,)), ((), ())), preferre...  5.86 us
  transfers between devices with their start and end apart: 2, of which 2 were waited for; matrix products, arithmetic and copies ran while one was open for 9% of the time, Pallas kernels for 0%

commit v1 on v0

--- a/solution.py
+++ b/solution.py
@@ -1,15 +1,114 @@
+import functools
+
 import jax
 import jax.numpy as jnp
 from jax import lax
+from jax.experimental import pallas as pl
+from jax.experimental.pallas import tpu as pltpu
 from jax.sharding import PartitionSpec as P
 
 D = 768
 HEADS = 16
-
-
-def broadcast(value, axis, source):
-    kept = jnp.where(lax.axis_index(axis) == source, value, 0).astype(value.dtype)
-    return lax.psum(kept, axis)
+MESH = pl.DeviceIdType.MESH
+
+
+def exchange(arrays, axis, n, scatter, collective_id):
+    count = len(arrays)
+
+    def kernel(*refs):
+        ins, outs = refs[:count], refs[count : 2 * count]
+        local_sem, send_sem, recv_sem = refs[2 * count :]
+        me = lax.axis_index(axis)
+        barrier = pltpu.get_barrier_semaphore()
+        for k in range(1, n):
+            pl.semaphore_signal(
+                barrier, inc=1, device_id={axis: lax.rem(me + k, n)}, device_id_type=MESH
+            )
+        own = []
+        for a in range(count):
+            src = ins[a].at[me] if scatter else ins[a]
+            own.append(pltpu.make_async_copy(src, outs[a].at[me], local_sem.at[a]))
+            own[-1].start()
+        pl.semaphore_wait(barrier, n - 1)
+        copies = []
+        for k in range(1, n):
+            peer = lax.rem(me + k, n)
+            for a in range(count):
+                copy = pltpu.make_async_remote_copy(
+                    src_ref=ins[a].at[peer] if scatter else ins[a],
+                    dst_ref=outs[a].at[me],
+                    send_sem=send_sem.at[a, k - 1],
+                    recv_sem=recv_sem.at[a, k - 1],
+                    device_id={axis: peer},
+                    device_id_type=MESH,
+                )
+                copy.start()
+                copies.append(copy)
+        for copy in own + copies:
+            copy.wait()
+
+    shapes = [x.shape if scatter else (n, *x.shape) for x in arrays]
+    return pl.pallas_call(
+        kernel,
+        out_shape=[jax.ShapeDtypeStruct(s, x.dtype) for s, x in zip(shapes, arrays)],
+        in_specs=[pl.BlockSpec(memory_space=pl.ANY)] * count,
+        out_specs=[pl.BlockSpec(memory_space=pl.ANY)] * count,
+        scratch_shapes=[
+            pltpu.SemaphoreType.DMA((count,)),
+            pltpu.SemaphoreType.DMA((count, n - 1)),
+            pltpu.SemaphoreType.DMA((count, n - 1)),
+        ],
+        compiler_params=pltpu.CompilerParams(collective_id=collective_id, has_side_effects=True),
+    )(*arrays)
+
+
+def spread(rows, n, per_row, offset_of, collective_id):
+    def kernel(in_ref, out_ref, local_sem, send_sem, recv_sem):
+        me = lax.axis_index("aa")
+        owner = lax.axis_index("ba") * offset_of // per_row
+        barrier = pltpu.get_barrier_semaphore()
+        for k in range(1, n):
+            pl.semaphore_signal(
+                barrier, inc=1, device_id={"aa": lax.rem(me + k, n)}, device_id_type=MESH
+            )
+        pl.semaphore_wait(barrier, n - 1)
+
+        def copy_to(k):
+            return pltpu.make_async_remote_copy(
+                src_ref=in_ref,
+                dst_ref=out_ref,
+                send_sem=send_sem.at[k - 1],
+                recv_sem=recv_sem,
+                device_id={"aa": lax.rem(me + k, n)},
+                device_id_type=MESH,
+            )
+
+        @pl.when(me == owner)
+        def _():
+            for k in range(1, n):
+                copy_to(k).start()
+            own = pltpu.make_async_copy(in_ref, out_ref, local_sem)
+            own.start()
+            own.wait()
+            for k in range(1, n):
+                copy_to(k).wait_send()
+
+        @pl.when(me != owner)
+        def _():
+            copy_to(1).wait_recv()
+
+    return pl.pallas_call(
+        kernel,
+        out_shape=jax.ShapeDtypeStruct(rows.shape, rows.dtype),
+        in_specs=[pl.BlockSpec(memory_space=pl.ANY)],
+        out_specs=pl.BlockSpec(memory_space=pl.ANY),
+        scratch_shapes=[
+            pltpu.SemaphoreType.DMA,
+            pltpu.SemaphoreType.DMA((n - 1,)),
+            pltpu.SemaphoreType.DMA,
+        ],
+        compiler_params=pltpu.CompilerParams(collective_id=collective_id, has_side_effects=True),
+    )(rows)
 
 
 def layer_norm(values, gain_row):
@@ -19,21 +118,17 @@
     return centered * lax.rsqrt(variance + 1e-05) * gain_row
 
 
-def widen(factor, head_dim):
-    return jnp.repeat(factor.T, head_dim, axis=1)
-
-
 def token_sums(local_ids, rounded_state, w_atom_token, tok_rows):
-    selector = (local_ids[:, None] == jnp.arange(tok_rows, dtype=jnp.int32)[None, :]).astype(
+    selector = (jnp.arange(tok_rows, dtype=jnp.int32)[:, None] == local_ids[None, :]).astype(
         jnp.bfloat16
     )
     hidden_atom = jax.nn.relu(
         jnp.dot(rounded_state, w_atom_token, preferred_element_type=jnp.float32)
     ).astype(jnp.bfloat16)
     sums = lax.dot_general(
-        selector, hidden_atom, (((0,), (0,)), ((), ())), preferred_element_type=jnp.float32
-    )
-    return (sums, jnp.sum(selector.astype(jnp.float32), axis=0))
+        selector, hidden_atom, (((1,), (0,)), ((), ())), preferred_element_type=jnp.float32
+    )
+    return (sums, jnp.sum(selector.astype(jnp.float32), axis=1))
 
 
 def project_start(tokens_start, gains, w_query_gate):
@@ -46,6 +141,8 @@
 
 
 def on_device(
+    n_aa,
+    n_ba,
     atom_cond,
     noisy_pos,
     noise_level,
@@ -80,22 +177,21 @@
     one_hot = (local_token[:, None] == jnp.arange(tok_rows, dtype=jnp.int32)[None, :]).astype(
         jnp.bfloat16
     )
-    group_state, group_ids = (
-        lax.all_gather(rounded_state, "ba", axis=0, tiled=True),
-        lax.all_gather(atom_token, "ba", axis=0, tiled=True),
-    )
+    group_state, group_ids = exchange(
+        [rounded_state, local_token.reshape(1, -1)], "ba", n_ba, False, 0
+    )
+    group_state = group_state.reshape(-1, group_state.shape[-1])
     summed, counts = token_sums(
-        group_ids - row_index * tok_rows, group_state, w_atom_token, tok_rows
+        group_ids.reshape(-1), group_state, w_atom_token, tok_rows
     )
     tokens_start = token_cond + summed / counts[:, None]
     normed, query_rows, gate_value = project_start(tokens_start, gains, w_query_gate)
     offset_row = col_index * block_cols % tok_rows
-    owner_row = col_index * block_cols // tok_rows
     slice_rows = lax.dynamic_slice_in_dim(normed, offset_row, block_cols, 0)
-    kv_local = jnp.dot(slice_rows, w_key_value, preferred_element_type=jnp.float32).astype(
-        jnp.bfloat16
-    )
-    key_value = broadcast(kv_local, "aa", owner_row)
+    block_rows = spread(slice_rows, n_aa, tok_rows, block_cols, 1)
+    key_value = jnp.dot(block_rows, w_key_value, preferred_element_type=jnp.float32).astype(
+        jnp.bfloat16
+    )
     key_heads = key_value[:, :D].reshape(block_cols, HEADS, head_dim)
     value_heads = key_value[:, D:].reshape(block_cols, HEADS, head_dim)
     query_heads = query_rows.reshape(tok_rows, HEADS, head_dim)
@@ -113,16 +209,26 @@
         value_heads,
         preferred_element_type=jnp.float32,
     ).reshape(tok_rows, D)
-    overall = lax.pmax(block_max, "ba")
-    factor = jnp.exp(block_max - overall)
-    out_all, total_all = (
-        lax.psum((partial_out * widen(factor, head_dim)).astype(jnp.bfloat16), "ba").astype(
-            jnp.float32
-        ),
-        lax.psum((block_total * factor).astype(jnp.bfloat16), "ba").astype(jnp.float32),
-    )
-    attended = out_all / widen(total_all, head_dim)
-    mixed_heads = (attended * gate_value.astype(jnp.float32)).astype(jnp.bfloat16)
+    own_rows = tok_rows // n_ba
+    stats = jnp.concatenate([block_max, block_total], axis=0).T
+    out_all, stats_all = exchange(
+        [
+            partial_out.astype(jnp.bfloat16).reshape(n_ba, own_rows, D),
+            stats.reshape(n_ba, own_rows, 2 * HEADS),
+        ],
+        "ba",
+        n_ba,
+        True,
+        2,
+    )
+    max_all, total_all = stats_all[:, :, :HEADS], stats_all[:, :, HEADS:]
+    factor = jnp.exp(max_all - jnp.max(max_all, axis=0, keepdims=True))
+    share = factor / jnp.sum(factor * total_all, axis=0, keepdims=True)
+    wide_share = jnp.repeat(share, head_dim, axis=2)
+    attended = jnp.sum(wide_share * out_all.astype(jnp.float32), axis=0)
+    gate_rows = lax.dynamic_slice_in_dim(gate_value, col_index * own_rows, own_rows, 0)
+    mixed_rows = (attended * gate_rows.astype(jnp.float32)).astype(jnp.bfloat16)
+    mixed_heads = exchange([mixed_rows], "ba", n_ba, False, 3)[0].reshape(tok_rows, D)
     tokens_mid = tokens_start + jnp.dot(mixed_heads, w_attn_out, preferred_element_type=jnp.float32)
     normed_mid = layer_norm(tokens_mid, gains[1]).astype(jnp.bfloat16)
     gate_up = jnp.dot(normed_mid, w_up, preferred_element_type=jnp.float32)
@@ -167,5 +273,6 @@
     )
     out_specs = (P(None, ("aa", "ba")), P("aa", None))
     return jax.shard_map(
-        on_device, mesh=mesh, in_specs=in_specs, out_specs=out_specs, check_vma=False
-    )
+        functools.partial(on_device, mesh.shape["aa"], mesh.shape["ba"]),
+        mesh=mesh, in_specs=in_specs, out_specs=out_specs, check_vma=False
+    )

time: 194 us -> 121 us (0.62)
  waiting for transfers between devices: 59.9 us -> 0 us
  blocking collectives: 57.7 us -> 0 us
  Pallas kernels: 0 us -> 47.9 us
  between operations: 15.1 us -> 1.66 us
  local copies, waits for them, and re-layouts: 18.8 us -> 28.5 us
  other arithmetic: 8.12 us -> 14.4 us
  matrix products: 33.5 us -> 27.6 us
    psum x2 -> x0, waiting for transfers between devices: 59.8 us -> none  [the longest x1 36.3 us: on_device(): lax.psum((partial_out * widen(factor, head_dim)).astype(jnp.bfloat16), 'ba')]
    pallas_call x0 -> x4, Pallas kernels: none -> 47.9 us  [the longest x3 30.3 us: exchange(): pl.pallas_call(kernel, out_shape=[jax.ShapeDtypeStruct(s, x.dtype) for s,...]
    all_gather x2 -> x0, blocking collectives: 22.6 us -> none  [the longest x1 12.2 us: on_device(): lax.all_gather(rounded_state, 'ba', axis=0, tiled=True)]
    pmax x1 -> x0, blocking collectives: 22.6 us -> none  [on_device(): overall = lax.pmax(block_max, 'ba')]
    psum x1 -> x0, blocking collectives: 12.5 us -> none  [on_device(): lax.psum((block_total * factor).astype(jnp.bfloat16), 'ba')]
    convert_element_type x1 -> x2, local copies, waits for them, and re-layouts: 0.95 us -> 4.72 us  [on_device(): partial_out.astype(jnp.bfloat16).reshape(n_ba, own_rows, D)]
    dot_general x2, matrix products: 8.76 us -> 6.38 us  [the longest x1 4.12 us: token_sums(): lax.dot_general(selector, hidden_atom, (((1,), (0,)), ((), ())), preferre...]
    reduce_sum x1 -> x3, other arithmetic: 1.36 us -> 3.51 us  [the longest x1 1.32 us: on_device(): attended = jnp.sum(wide_share * out_all.astype(jnp.float32), axis=0)]
  transfers between devices with their start and end apart: 2 -> 0, of which waited for: 2 -> 0; matrix products, arithmetic and copies ran while one was open for 9% -> 0% of each run, Pallas kernels for 0% -> 0%
where the time goes in v1:
time: 121 us; the launch traced here: 120 us
  Pallas kernels  47.9 us (40%)
  local copies, waits for them, and re-layouts  28.5 us (24%)
  matrix products  27.6 us (23%)
  other arithmetic  14.4 us (12%)
  between operations  1.66 us (1%)
    pallas_call x3, Pallas kernels, exchange(): pl.pallas_call(kernel, out_shape=[jax.ShapeDtypeStruct(s, x.dtype) for s,...  30.3 us
    pallas_call x1, Pallas kernels, spread(): pl.pallas_call(kernel, out_shape=jax.ShapeDtypeStruct(rows.shape, rows.dt...  17.6 us
    dot_general x1, matrix products, on_device(): jnp.einsum('hc,ijc->hij', pair_bias_weight, pair, preferred_element_type=...  6.97 us
    convert_element_type x2, local copies, waits for them, and re-layouts, on_device(): partial_out.astype(jnp.bfloat16).reshape(n_ba, own_rows, D)  4.72 us
    dot_general x1, matrix products, token_sums(): lax.dot_general(selector, hidden_atom, (((1,), (0,)), ((), ())), preferre...  4.12 us
    unnamed x42, local copies, waits for them, and re-layouts  4.06 us
    dot_general x1, matrix products, on_device(): gate_up = jnp.dot(normed_mid, w_up, preferred_element_type=jnp.float32)  3.95 us
    reshape x1, local copies, waits for them, and re-layouts, on_device(): wide_share = jnp.repeat(share, head_dim, axis=2)  3.03 us

profile of v1, /device:TPU:0, one launch (start us, length us, event | category | flops | bytes accessed | tf_op | source)
XLA Modules:
  0.0 120.0 jit_solution(16315514768770571278)
XLA Ops:
  3.5 1.8 %fusion.25.refs_0_ = bf16[384,128]{1,0:T(8,128)(2,1)} fusion(f32[384,128]{1,0:T(8,128)} %param.17, f32[128]{0:T(128)S(1)} %get-tuple-element.19, f32[384]{0:T(512)S(1)} %get-tuple-element.14, f32[128]{0:T(128)S(1)} %get-tuple-element.20, f32[384]{0:T(512)S(1)} %get-tuple-element.15, f32[128]{0:T(128)S(1)} %get-tuple-element.18, f32[384]{0:T(512)S(1)} %get-tuple-element.13), kind=kLoop, calls=%fused_computation.47 | loop fusion | flops 344064 | bytes 301056 | tf_op jit(solution)/shard_map/convert_element_type | solution.py:175
  7.1 13.6 %shard_map.176 = (bf16[8,384,128]{2,1,0:T(8,128)(2,1)}, s32[8,1,384]{2,1,0:T(1,128)}) custom-call(bf16[384,128]{1,0:T(8,128)(2,1)} %fusion.25.refs_0_, s32[1,384]{1,0:T(1,128)} %reshape.89.refs_1_), custom_call_target="tpu_custom_call" | custom-call | tf_op jit(solution)/shard_map/pallas_call | solution.py:51
  21.8 4.1 %fusion.38 = (f32[256]{0:T(256)S(1)}, f32[256,768]{1,0:T(8,128)S(1)}) fusion(f32[256,768]{1,0:T(8,128)} %param.21, f32[256]{0:T(256)S(1)} %convert_reduce_fusion, bf16[3072,128]{1,0:T(8,128)(2,1)} %bitcast.53, bf16[128,768]{1,0:T(8,128)(2,1)} %param.26, s32[3072]{0:T(1024)} %bitcast.52), kind=kOutput, calls=%fused_computation.84 | convolution fusion | flops 1818033920 | bytes 2570240 | tf_op jit(solution)/shard_map/dot_general | solution.py:128
  27.7 17.6 %shard_map.177 = bf16[128,768]{1,0:T(8,128)(2,1)} custom-call(bf16[128,768]{1,0:T(8,128)(2,1)} %constant_dynamic-slice_fusion.in_ref), custom_call_target="tpu_custom_call" | custom-call | tf_op jit(solution)/shard_map/pallas_call | solution.py:100
  45.3 2.3 %convolution_convert_fusion = bf16[128,1536]{1,0:T(8,128)(2,1)S(1)} fusion(bf16[128,768]{1,0:T(8,128)(2,1)} %shard_map.177, bf16[768,1536]{1,0:T(8,128)(2,1)} %param.28), kind=kOutput, calls=%fused_computation.5 | convolution fusion | flops 302186496 | bytes 2949120 | tf_op jit(solution)/shard_map/dot_general | solution.py:192
  48.4 1.7 %copy.43 = bf16[128,768]{0,1:T(8,128)(2,1)} copy(bf16[128,768]{1,0:T(8,128)(2,1)} %get-tuple-element.17) | data formatting | bytes 393216 | tf_op jit(solution)/shard_map/slice | solution.py:196
  50.1 7.0 %fusion.33 = f32[16,256,128]{2,0,1:T(8,128)} fusion(bf16[256,128,128]{2,1,0:T(8,128)(2,1)} %param.22, bf16[16,128]{1,0:T(8,128)(2,1)S(1)} %copy-done.14), kind=kOutput, calls=%fused_computation.59 | convolution fusion | flops 134217728 | bytes 10489856 | tf_op jit(solution)/shard_map/hc,ijc->hij/dot_general | solution.py:200
  57.1 3.0 %copy.46 = f32[16,256,128]{1,2,0:T(8,128)} copy(f32[16,256,128]{2,0,1:T(8,128)} %fusion.33) | data formatting | bytes 4194304 | tf_op jit(solution)/shard_map/hc,ijc->hij/dot_general | solution.py:200
  63.9 1.7 %copy.45 = bf16[128,768]{0,1:T(8,128)(2,1)} copy(bf16[128,768]{1,0:T(8,128)(2,1)} %get-tuple-element.16) | data formatting | bytes 393216 | tf_op jit(solution)/shard_map/slice | solution.py:195
  65.7 2.3 %fusion.39 = (f32[16,256]{1,0:T(8,128)S(1)}, f32[16,256,128]{1,2,0:T(8,128)S(1)}) fusion(f32[16,256,128]{1,2,0:T(8,128)} %copy.46, bf16[256,16,48]{0,2,1:T(8,128)(2,1)S(1)} %bitcast.46, bf16[128,16,48]{0,2,1:T(8,128)(2,1)} %bitcast.48), kind=kOutput, calls=%fused_computation.85 | convolution fusion | flops 51900416 | bytes 4800512 | tf_op jit(solution)/shard_map/ihd,jhd->hij/dot_general | solution.py:198
  67.9 1.3 %copy-done.1 = f32[16,256,128]{1,2,0:T(8,128)} copy-done((f32[16,256,128]{1,2,0:T(8,128)}, f32[16,256,128]{1,2,0:T(8,128)S(1)}, u32[]{:S(2)}) %copy-start.1) | copy-done | bytes 2097176
  69.8 1.8 %copy.48 = bf16[256,16,48]{2,1,0:T(8,128)(2,1)} copy(bf16[256,16,48]{0,2,1:T(8,128)(2,1)S(1)} %fusion.6) | data formatting | bytes 786432 | tf_op jit(solution)/shard_map/convert_element_type | solution.py:216
  71.6 2.9 %convert_element_type.69.refs_0_ = bf16[8,32,768]{2,1,0:T(8,128)(2,1)} reshape(bf16[256,16,48]{2,1,0:T(8,128)(2,1)} %copy.48) | data formatting | bytes 786432 | tf_op jit(solution)/shard_map/convert_element_type | solution.py:216
  74.5 1.9 %fusion.2 = f32[16,256]{1,0:T(8,128)S(1)} fusion(f32[16,256,128]{1,2,0:T(8,128)} %copy-done.1, f32[16,256]{1,0:T(8,128)S(1)} %get-tuple-element.23), kind=kLoop, calls=%fused_computation.8 | loop fusion | flops 1044480 | bytes 2129920 | tf_op jit(solution)/shard_map/reduce_sum | solution.py:205
  77.2 8.4 %shard_map.178 = (bf16[8,32,768]{2,1,0:T(8,128)(2,1)}, f32[8,32,32]{2,1,0:T(8,128)}) custom-call(bf16[8,32,768]{2,1,0:T(8,128)(2,1)} %convert_element_type.69.refs_0_, f32[8,32,32]{2,1,0:T(8,128)} %bitcast.50), custom_call_target="tpu_custom_call" | custom-call | tf_op jit(solution)/shard_map/pallas_call | solution.py:51
  88.5 2.0 %broadcast_in_dim.2 = f32[8,32,16,48]{3,2,1,0:T(8,128)} broadcast(f32[8,32,16]{2,1,0:T(8,128)S(1)} %fusion.26), dimensions={0,1,2} | broadcast | bytes 802816 | tf_op jit(solution)/shard_map/broadcast_in_dim | solution.py:227
  90.5 3.0 %reshape.95 = f32[8,32,768]{2,1,0:T(8,128)} reshape(f32[8,32,16,48]{3,2,1,0:T(8,128)} %broadcast_in_dim.2) | data formatting | bytes 1572864 | tf_op jit(solution)/shard_map/reshape | solution.py:227
  94.8 2.1 %slice.75 = f32[256,768]{1,0:T(8,128)} slice(f32[256,1536]{1,0:T(8,128)} %copy-done.2), slice={[0:256], [768:1536]} | slice | bytes 1572864 | tf_op jit(solution)/shard_map/slice | solution.py:139
  96.9 1.5 %multiply_convert_fusion.8.refs_0_ = bf16[32,768]{1,0:T(8,128)(2,1)} fusion(f32[32,768]{1,0:T(8,128)S(1)} %multiply_reduce_fusion.2, f32[256,768]{1,0:T(8,128)} %slice.75, s32[]{:T(128)S(6)} %select_n.15), kind=kLoop, calls=%fused_computation.56 | loop fusion | flops 172032 | bytes 245764 | tf_op jit(solution)/shard_map/convert_element_type | solution.py:230
  98.4 8.3 %shard_map.179 = bf16[8,32,768]{2,1,0:T(8,128)(2,1)} custom-call(bf16[32,768]{1,0:T(8,128)(2,1)} %multiply_convert_fusion.8.refs_0_), custom_call_target="tpu_custom_call" | custom-call | tf_op jit(solution)/shard_map/pallas_call | solution.py:51
  106.8 2.0 %fusion.40 = (f32[256]{0:T(256)S(1)}, f32[256,768]{1,0:T(8,128)S(1)}) fusion(f32[256,768]{1,0:T(8,128)S(1)} %get-tuple-element.22, bf16[256,768]{1,0:T(8,128)(2,1)} %bitcast.47, bf16[768,768]{1,0:T(8,128)(2,1)} %param.29), kind=kOutput, calls=%fused_computation.86 | convolution fusion | flops 302382848 | bytes 3146752 | tf_op jit(solution)/shard_map/dot_general | solution.py:232
  109.0 4.0 %fusion.14 = f32[256,3072]{1,0:T(8,128)S(1)} fusion(bf16[768,3072]{1,0:T(8,128)(2,1)} %param.30, f32[256,768]{1,0:T(8,128)S(1)} %get-tuple-element.26, f32[768]{0:T(1024)S(1)} %copy-done.16, f32[256]{0:T(256)S(1)} %add_rsqrt_fusion.2, f32[256]{0:T(256)S(1)} %broadcast_multiply_fusion.3), kind=kOutput, calls=%fused_computation.33 | convolution fusion | flops 1208745984 | bytes 8655872 | tf_op jit(solution)/shard_map/dot_general | solution.py:234
  115.3 2.2 %fusion.42 = (f32[384]{0:T(512)}, f32[384,128]{1,0:T(8,128)S(1)}) fusion(bf16[768,128]{1,0:T(8,128)(2,1)} %param.32, f32[256,768]{1,0:T(8,128)S(1)} %get-tuple-element.28, f32[768]{0:T(1024)} %get-tuple-element.10, f32[256]{0:T(256)} %add_rsqrt_fusion.1, f32[256]{0:T(256)} %copy-done.15, s32[384]{0:T(512)} %copy-done.12, f32[128]{0:T(128)} %copy-done.18, ...), kind=kOutput, calls=%fused_computation.88 | convolution fusion | flops 76807808 | bytes 1390592 | tf_op jit(solution)/shard_map/dot_general | solution.py:244
  118.5 1.6 %fusion.10 = f32[3,384]{1,0:T(4,128)} fusion(bf16[3,128]{1,0:T(4,128)(2,1)} %param.33, f32[384,128]{1,0:T(8,128)S(1)} %get-tuple-element.30, f32[384]{0:T(512)S(1)} %add_rsqrt_fusion, f32[384]{0:T(512)S(1)} %broadcast_multiply_fusion.1, f32[3,384]{1,0:T(4,128)S(1)} %copy-done.6, f32[]{:T(128)S(6)} %mul.238, f32[]{:T(128)S(6)} %mul.187), kind=kOutput, calls=%fused_computation.23 | convolution fusion | flops 445824 | bytes 209672 | tf_op jit(solution)/shard_map/dot_general | solution.py:247
  (74 shorter events, 20.4 us)
Async XLA Ops:
  0.6 59.4 %copy-start = (bf16[768,1536]{1,0:T(8,128)(2,1)S(1)}, bf16[768,1536]{1,0:T(8,128)(2,1)}, u32[]{:S(2)}) copy-start(bf16[768,1536]{1,0:T(8,128)(2,1)} %param.27) | copy-start | bytes 7077892
  1.5 20.3 %copy-start.17 = (f32[128]{0:T(128)}, f32[128]{0:T(128)S(1)}, u32[]{:S(2)}) copy-start(f32[128]{0:T(128)S(1)} %get-tuple-element.18) | copy-start | bytes 1540
  1.5 20.3 %copy-start.18 = (f32[128]{0:T(128)}, f32[128]{0:T(128)S(1)}, u32[]{:S(2)}) copy-start(f32[128]{0:T(128)S(1)} %get-tuple-element.19) | copy-start | bytes 1540
  1.5 20.3 %copy-start.19 = (f32[128]{0:T(128)}, f32[128]{0:T(128)S(1)}, u32[]{:S(2)}) copy-start(f32[128]{0:T(128)S(1)} %get-tuple-element.20) | copy-start | bytes 1540
  2.9 0.6 copy-start.7
  2.9 2.3 %copy-start.9 = (f32[384]{0:T(512)}, f32[384]{0:T(512)S(1)}, u32[]{:S(2)}) copy-start(f32[384]{0:T(512)S(1)} %get-tuple-element.14) | copy-start | bytes 4612
  3.0 2.3 %copy-start.11 = (f32[384]{0:T(512)}, f32[384]{0:T(512)S(1)}, u32[]{:S(2)}) copy-start(f32[384]{0:T(512)S(1)} %get-tuple-element.15) | copy-start | bytes 4612
  6.0 0.6 copy-start.12
  21.8 4.1 %copy-start.13 = (f32[3,768]{1,0:T(4,128)S(1)}, f32[3,768]{1,0:T(4,128)}, u32[]{:S(2)}) copy-start(f32[3,768]{1,0:T(4,128)} %param.24) | copy-start | bytes 27652
  45.3 4.8 %copy-start.14 = (bf16[16,128]{1,0:T(8,128)(2,1)S(1)}, bf16[16,128]{1,0:T(8,128)(2,1)}, u32[]{:S(2)}) copy-start(bf16[16,128]{1,0:T(8,128)(2,1)} %param.23) | copy-start | bytes 12292
  60.8 1.2 copy-start.2
  65.7 3.6 %copy-start.4 = (bf16[128,768]{0,1:T(8,128)(2,1)S(1)}, bf16[128,768]{0,1:T(8,128)(2,1)}, u32[]{:S(2)}) copy-start(bf16[128,768]{0,1:T(8,128)(2,1)} %copy.43) | copy-start | bytes 589828
  67.9 1.4 %copy-start.1 = (f32[16,256,128]{1,2,0:T(8,128)}, f32[16,256,128]{1,2,0:T(8,128)S(1)}, u32[]{:S(2)}) copy-start(f32[16,256,128]{1,2,0:T(8,128)S(1)} %get-tuple-element.24) | copy-start | bytes 6291460
  98.4 10.6 %copy-start.16 = (f32[768]{0:T(1024)S(1)}, f32[768]{0:T(1024)}, u32[]{:S(2)}) copy-start(f32[768]{0:T(1024)} %get-tuple-element.12) | copy-start | bytes 9220
  109.0 4.0 %copy-start.20 = (bf16[1536,768]{1,0:T(8,128)(2,1)S(1)}, bf16[1536,768]{1,0:T(8,128)(2,1)}, u32[]{:S(2)}) copy-start(bf16[1536,768]{1,0:T(8,128)(2,1)} %param.31) | copy-start | bytes 7077892
  113.0 2.3 %copy-start.5 = (f32[384,128]{1,0:T(8,128)S(1)}, f32[384,128]{1,0:T(8,128)}, u32[]{:S(2)}) copy-start(f32[384,128]{1,0:T(8,128)} %param.17) | copy-start | bytes 589828
  113.0 2.3 %copy-start.8 = (f32[384]{0:T(512)S(1)}, f32[384]{0:T(512)}, u32[]{:S(2)}) copy-start(f32[384]{0:T(512)} %copy-done.7) | copy-start | bytes 4612
  113.0 2.3 %copy-start.10 = (f32[384]{0:T(512)S(1)}, f32[384]{0:T(512)}, u32[]{:S(2)}) copy-start(f32[384]{0:T(512)} %copy-done.9) | copy-start | bytes 4612
  114.1 5.9 %copy-start.3 = (f32[256,768]{1,0:T(8,128)}, f32[256,768]{1,0:T(8,128)S(1)}, u32[]{:S(2)}) copy-start(f32[256,768]{1,0:T(8,128)S(1)} %get-tuple-element.28) | copy-start | bytes 2359300
  114.1 4.4 %copy-start.6 = (f32[3,384]{1,0:T(4,128)S(1)}, f32[3,384]{1,0:T(4,128)}, u32[]{:S(2)}) copy-start(f32[3,384]{1,0:T(4,128)} %param.18) | copy-start | bytes 13828
  114.1 0.6 copy-start.15
